TPU v7x, 32 devices: a whole 2x2x4 slice. The times are simulated.
32 devices in a mesh: img: 8 (over z, y), rep: 4 (over x, core).
Axes of the slice: x: 2, y: 2, z: 4, core: 2. Of those that a mesh axis runs over, the one named last changes fastest.
Arguments:
- descriptors: bfloat16 [16, 256, 1024], P('img', 'rep'), may hold values from -0.5 to 0.5
- cell_counts: int32 [16, 256], P('img', 'rep'), may hold values from 1 to 8
- pair_images: int32 [64, 2], P('img'), may hold values from 0 to 15, as said below
- query_cells: int32 [64, 16], P('img'), may hold values from 0 to 255
- cand_cells: int32 [64, 4, 16], P('img', 'rep'), may hold values from 0 to 255, as said below
- cand_counts: int32 [64, 4], P('img', 'rep'), may hold values from 8 to 16, as said below
Outputs:
- matches: float32 [64, 2, 128], P('img')
- image_score: float32 [16], P('img')
Inputs may be any that keep to these rules, and one draw needn't show every extreme that they name: `pair_images`: the pairs are numbered by blocks of 8: pair k * 8 + j has its first image among images k * 2 to k * 2 + 1 and its second among images j * 2 to j * 2 + 1; the two images of a pair differ. cand_cells[p, r, s] lies in quarter r, between r * 64 and r * 64 + 63; cells may repeat. `cand_counts`: every count is 8 or 16, and every draw holds at least one count of 16.
All inputs are finite; a program needn't handle non-finite values.
Results may differ from a plain program's by a relative error of at most 0.0003.
Values may be sent and summed in bfloat16 or wider, within the bound.
A program may use at most 64 MiB of HBM per device.

v0:
```python
import jax
import jax.numpy as jnp
from jax import lax
from jax.sharding import PartitionSpec as P

DESC = 128
KP = 8
distant = 1000000000.0
group_size = 8


def joined(shard, axis, combine):
    everything = jax.tree.map(lambda part: lax.all_gather(part, axis), shard)
    leading = jax.tree.map(lambda part: part[0], everything)

    def turn(k, so_far):
        return combine(so_far, jax.tree.map(lambda part: part[k], everything))

    return lax.fori_loop(1, lax.axis_size(axis), turn, leading)


def nearest(queries, blocks, block_counts, live_cells):
    pairs = queries.shape[0]
    slots = blocks.shape[1]
    cands = blocks.reshape(pairs, slots * KP, DESC)
    cell_live = jnp.arange(slots, dtype=jnp.int32)[None, :] < live_cells[:, None]
    slot_live = (
        jnp.arange(KP, dtype=jnp.float32)[None, None, :]
        < block_counts.astype(jnp.float32)[:, :, None]
    )
    clive = (cell_live[:, :, None] & slot_live).reshape(pairs, slots * KP)
    groups = pairs // group_size

    def one_group(packed):
        query_part, cand_part, live_part = packed
        qwide = query_part.astype(jnp.float32)
        cwide = cand_part.astype(jnp.float32)
        qnorm = jnp.sum(qwide * qwide, axis=2)
        cnorm = jnp.sum(cwide * cwide, axis=2)
        inner = jnp.einsum(
            "pqd,pcd->pqc", query_part, cand_part, preferred_element_type=jnp.float32
        )
        dist = qnorm[:, :, None] + cnorm[:, None, :] - 2.0 * inner
        dist = jnp.where(live_part[:, None, :], dist, jnp.float32(distant))
        lowest = -lax.top_k(-dist, 2)[0]
        return (lowest[..., 0], lowest[..., 1])

    packed = (
        queries.reshape(groups, group_size, -1, DESC),
        cands.reshape(groups, group_size, -1, DESC),
        clive.reshape(groups, group_size, -1),
    )
    best, runner = lax.map(one_group, packed)
    return (best.reshape(pairs, -1), runner.reshape(pairs, -1))


def keep_two(left, right):
    low = jnp.minimum(left[0], right[0])
    high = jnp.minimum(jnp.maximum(left[0], right[0]), jnp.minimum(left[1], right[1]))
    return (low, high)


def on_device(descriptors, cell_counts, pair_images, query_cells, cand_cells, cand_counts):
    img_dev, share, width = descriptors.shape
    peers = lax.axis_size("img")
    whole, whole_counts = (
        lax.all_gather(descriptors, "rep", axis=1, tiled=True),
        lax.all_gather(cell_counts.astype(jnp.bfloat16), "rep", axis=1, tiled=True),
    )
    cells = whole.shape[1]
    first_local = pair_images[:, 0] % img_dev
    second_local = pair_images[:, 1] % img_dev
    query_rows = (first_local[:, None] * cells + query_cells).reshape(-1)
    queries = jnp.take(whole.reshape(img_dev * cells, width), query_rows, axis=0).reshape(
        peers, -1, DESC
    )
    query_counts = jnp.take(whole_counts.reshape(img_dev * cells), query_rows).reshape(peers, -1)
    qlive = (
        jnp.arange(KP, dtype=jnp.float32)[None, None, :]
        < query_counts.astype(jnp.float32)[:, :, None]
    ).reshape(peers, -1)
    lists = cand_cells[:, 0, :]
    live_cells = cand_counts[:, 0]
    local_rows = descriptors.reshape(img_dev * share, width)
    local_counts = cell_counts.reshape(img_dev * share)
    asked, asked_image = (
        lax.all_to_all(lists, "img", split_axis=0, concat_axis=0, tiled=True),
        lax.all_to_all(second_local, "img", split_axis=0, concat_axis=0, tiled=True),
    )
    rows = (asked_image[:, None] * share + asked % share).reshape(-1)
    blocks = jnp.take(local_rows, rows, axis=0).reshape(peers, -1, width)
    block_counts = jnp.take(local_counts, rows).reshape(peers, -1).astype(jnp.bfloat16)
    blocks, block_counts = (
        lax.all_to_all(blocks, "img", split_axis=0, concat_axis=0, tiled=True),
        lax.all_to_all(block_counts, "img", split_axis=0, concat_axis=0, tiled=True),
    )
    best, runner = nearest(queries, blocks, block_counts, live_cells)
    best, runner = joined((best, runner), "rep", keep_two)
    best = jnp.where(qlive, best, jnp.float32(0.0))
    runner = jnp.where(qlive, runner, jnp.float32(0.0))
    matches = jnp.stack([best, runner], axis=1)
    margin = jnp.where(qlive, (runner - best) / (runner + 1.0), jnp.float32(0.0))
    score = jnp.sum(margin, axis=1) / jnp.sum(qlive.astype(jnp.float32), axis=1)
    arrived = lax.all_to_all(score, "img", split_axis=0, concat_axis=0, tiled=True)
    image_ids = jnp.arange(img_dev, dtype=jnp.int32)
    own_part = jnp.sum(
        jnp.where(first_local[:, None] == image_ids[None, :], score[:, None], jnp.float32(0.0)),
        axis=0,
    )
    other_part = jnp.sum(
        jnp.where(asked_image[:, None] == image_ids[None, :], arrived[:, None], jnp.float32(0.0)),
        axis=0,
    )
    return (matches, own_part + other_part)


def solution(mesh):
    in_specs = (
        P("img", "rep", None),
        P("img", "rep"),
        P("img", None),
        P("img", None),
        P("img", "rep", None),
        P("img", "rep"),
    )
    out_specs = (P("img", None, None), P("img"))
    return jax.shard_map(
        on_device, mesh=mesh, in_specs=in_specs, out_specs=out_specs, check_vma=False
    )
```

profile of v0, /device:TPU:0, one launch (start us, length us, event | category | flops | bytes accessed | tf_op | source)
XLA Modules:
  0.0 107.9 jit_solution(14698842884387432103)
XLA Ops:
  7.2 0.7 all-gather.5.cloned.1.call-update
  7.9 0.7 copy.43
  8.6 7.3 %all-to-all-start = ((s32[8,1,1]{2,1,0:T(1,128)}), s32[8,1,1]{2,1,0:T(1,128)S(1)}, u32[]{:S(2)}, u32[]{:S(2)}) async-start(s32[8,1,1]{2,1,0:T(1,128)} %copy.43), calls=%async_computation | async-start | bytes 8192 | tf_op jit(solution)/shard_map/all_to_all | solution.py:88
  15.9 0.7 copy-done.3
  16.6 0.7 copy-done.4
  17.3 5.0 %all-gather.2 = bf16[4,64,2]{1,2,0:T(2,128)(2,1)S(1)} all-gather(bf16[1,64,2]{1,2,0:T(2,128)(2,1)S(1)} %convert_bitcast_fusion), channel_id=1, replica_groups=mesh['img'=8,'rep'=4] {'rep'}, dimensions={0}, use_global_device_ids=true | all-gather | bytes 1280 | tf_op jit(solution)/shard_map/all_gather | solution.py:68
  22.5 0.6 copy-done.1
  23.2 1.3 %gather_fusion = bf16[128]{0:T(256)(128)(2,1)S(1)} fusion(bf16[512]{0:T(512)(128)(2,1)S(1)} %bitcast.56, s32[1024]{0:T(1024)S(1)} %pad_clamp_fusion.1), kind=kCustom, calls=%fused_computation | custom fusion | bytes 1024 | tf_op jit(solution)/shard_map/jit(_take)/gather | solution.py:77
  24.8 6.0 %all-to-all-start.1 = ((s32[8,1,16]{2,1,0:T(1,128)}), s32[8,1,16]{2,1,0:T(1,128)S(1)}, u32[]{:S(2)}, u32[]{:S(2)}) async-start(s32[8,1,16]{2,1,0:T(1,128)} %param.12), calls=%async_computation.1 | async-start | bytes 8192 | tf_op jit(solution)/shard_map/all_to_all | solution.py:87
  30.8 0.2 reduce.1
  31.2 6.0 %all-to-all-done.1 = s32[8,1,16]{2,1,0:T(1,128)S(1)} async-done(((s32[8,1,16]{2,1,0:T(1,128)}), s32[8,1,16]{2,1,0:T(1,128)S(1)}, u32[]{:S(2)}, u32[]{:S(2)}) %all-to-all-start.1) | async-done | bytes 544 | tf_op jit(solution)/shard_map/all_to_all | solution.py:87
  37.2 0.5 broadcast.286
  37.7 0.7 reduce.6
  38.5 1.2 %gather_fusion.1 = s32[128]{0:T(128)S(1)} fusion(s32[128]{0:T(128)S(1)} %reshape.315, s32[1024]{0:T(1024)S(1)} %pad_clamp_fusion), kind=kCustom, calls=%fused_computation.1 | custom fusion | bytes 1536 | tf_op jit(solution)/shard_map/jit(_take)/gather | solution.py:92
  39.9 0.6 copy.47
  40.5 3.3 %all-to-all-start.2 = ((bf16[8,1,16]{2,1,0:T(2,128)(2,1)}), bf16[8,1,16]{2,1,0:T(2,128)(2,1)S(1)}, u32[]{:S(2)}, u32[]{:S(2)}) async-start(bf16[8,1,16]{2,1,0:T(2,128)(2,1)} %copy.47), calls=%async_computation.2 | async-start | bytes 8192 | tf_op jit(solution)/shard_map/all_to_all | solution.py:95
  43.8 0.9 gather_fusion.3
  44.7 0.8 broadcast_select_fusion
  45.6 4.6 %all-to-all-done.2 = bf16[8,1,16]{2,1,0:T(2,128)(2,1)S(1)} async-done(((bf16[8,1,16]{2,1,0:T(2,128)(2,1)}), bf16[8,1,16]{2,1,0:T(2,128)(2,1)S(1)}, u32[]{:S(2)}, u32[]{:S(2)}) %all-to-all-start.2) | async-done | bytes 288 | tf_op jit(solution)/shard_map/all_to_all | solution.py:95
  50.1 3.4 %all-to-all-start.3 = ((bf16[8,16,1024]{2,1,0:T(8,128)(2,1)}), bf16[8,16,1024]{2,1,0:T(8,128)(2,1)S(1)}, u32[]{:S(2)}, u32[]{:S(2)}) async-start(bf16[8,16,1024]{2,1,0:T(8,128)(2,1)} %broadcast_select_fusion), calls=%async_computation.3 | async-start | bytes 524288 | tf_op jit(solution)/shard_map/all_to_all | solution.py:94
  53.6 0.2 convert_reduce_fusion
  54.0 0.1 broadcast_in_dim.111
  54.2 0.1 and.97
  54.3 0.1 lt.166
  54.6 7.1 %all-to-all-done.3 = bf16[8,16,1024]{2,1,0:T(8,128)(2,1)S(1)} async-done(((bf16[8,16,1024]{2,1,0:T(8,128)(2,1)}), bf16[8,16,1024]{2,1,0:T(8,128)(2,1)S(1)}, u32[]{:S(2)}, u32[]{:S(2)}) %all-to-all-start.3) | async-done | bytes 262176 | tf_op jit(solution)/shard_map/all_to_all | solution.py:94
  61.7 0.1 squeeze.46
  61.8 0.2 multiply_reduce_fusion
  62.1 2.4 %gather_fusion.2 = bf16[128,1024]{1,0:T(8,128)(2,1)S(1)} fusion(bf16[512,1024]{1,0:T(8,128)(2,1)} %bitcast.58, s32[1024]{0:T(1024)S(1)} %pad_clamp_fusion.1), kind=kCustom, calls=%fused_computation.2 | custom fusion | bytes 524800 | tf_op jit(solution)/shard_map/jit(_take)/gather | solution.py:74
  64.5 0.1 gather.29
  64.6 0.3 convolution_multiply_fusion
  64.9 2.6 %fusion.5 = f32[8,128,128]{2,1,0:T(8,128)S(1)} fusion(f32[8,128,128]{2,1,0:T(8,128)S(1)} %convolution_multiply_fusion, f32[8,128]{1,0:T(8,128)S(1)} %multiply_reduce_fusion, pred[8,128]{1,0:T(8,128)(4,1)S(1)} %compare_and_fusion.1, bf16[8,128,128]{2,1,0:T(8,128)(2,1)S(1)} %gather.29, pred[8,128]{1,0:T(8,128)(4,1)S(1)} %broadcast_in_dim.111), kind=kOutput, calls=%fused_computation.12 | output fusion | flops 918655 | bytes 1316864 | tf_op jit(solution)/shard_map/while/body/eval_jaxpr/add | solution.py:43
  67.5 0.2 copy.55
  67.8 10.5 %top_k.9 = (f32[8,128,128]{1,2,0:T(8,128)S(1)}, s32[8,128,128]{1,2,0:T(8,128)}) sort(f32[8,128,128]{1,2,0:T(8,128)S(1)} %copy.55, s32[8,128,128]{1,2,0:T(8,128)S(1)} %iota.21.clone), dimensions={2}, to_apply=%region_2.3 | sort | flops 2228224 | bytes 2097152 | tf_op jit(solution)/shard_map/while/body/eval_jaxpr/top_k | solution.py:45
  78.3 0.2 copy.57
  78.5 0.2 fusion.23
  78.7 0.2 copy.51
  78.9 0.2 copy.49
  79.1 5.2 %all-gather = f32[32,128,1]{1,2,0:T(1,128)S(1)} all-gather(f32[8,128,1]{1,2,0:T(1,128)S(1)} %copy.49), channel_id=2, replica_groups=mesh['img'=8,'rep'=4] {'rep'}, dimensions={0}, use_global_device_ids=true | all-gather | bytes 20480 | tf_op jit(solution)/shard_map/all_gather | solution.py:13
  84.3 5.2 %all-gather.1 = f32[32,128,1]{1,2,0:T(1,128)S(1)} all-gather(f32[8,128,1]{1,2,0:T(1,128)S(1)} %copy.51), channel_id=3, replica_groups=mesh['img'=8,'rep'=4] {'rep'}, dimensions={0}, use_global_device_ids=true | all-gather | bytes 20480 | tf_op jit(solution)/shard_map/all_gather | solution.py:13
  89.5 0.1 select_reduce_fusion
  89.7 0.1 fusion.13
  89.8 0.7 copy.53
  90.5 3.3 %all-to-all-start.4 = ((f32[8,1,1]{2,1,0:T(1,128)}), f32[8,1,1]{2,1,0:T(1,128)S(1)}, u32[]{:S(2)}, u32[]{:S(2)}) async-start(f32[8,1,1]{2,1,0:T(1,128)} %copy.53), calls=%async_computation.4 | async-start | bytes 8192 | tf_op jit(solution)/shard_map/all_to_all | solution.py:104
  93.8 0.6 copy.54
  94.4 5.8 %all-to-all-done.4 = f32[8,1,1]{2,1,0:T(1,128)S(1)} async-done(((f32[8,1,1]{2,1,0:T(1,128)}), f32[8,1,1]{2,1,0:T(1,128)S(1)}, u32[]{:S(2)}, u32[]{:S(2)}) %all-to-all-start.4) | async-done | bytes 64 | tf_op jit(solution)/shard_map/all_to_all | solution.py:104
  100.3 0.1 reduce.3
  100.4 0.1 fusion.14
  100.5 0.5 add.234
  (53 shorter events, 1.9 us)
Async XLA Ops:
  7.2 0.7 copy-start.2
  7.2 54.9 %all-gather.5.cloned.1.call-start = ((), (), s32[]{:S(2)}) async-start(), calls=%async_computation.5 | async-start | bytes 1310720 | tf_op jit(solution)/shard_map/all_gather | solution.py:67
  8.6 16.1 %all-to-all-start = ((s32[8,1,1]{2,1,0:T(1,128)}), s32[8,1,1]{2,1,0:T(1,128)S(1)}, u32[]{:S(2)}, u32[]{:S(2)}) async-start(s32[8,1,1]{2,1,0:T(1,128)} %copy.43), calls=%async_computation | async-start | bytes 8192 | tf_op jit(solution)/shard_map/all_to_all | solution.py:88
  15.9 0.7 copy-start.3
  16.6 0.7 copy-start.4
  22.4 0.7 copy-start.1
  24.8 12.4 %all-to-all-start.1 = ((s32[8,1,16]{2,1,0:T(1,128)}), s32[8,1,16]{2,1,0:T(1,128)S(1)}, u32[]{:S(2)}, u32[]{:S(2)}) async-start(s32[8,1,16]{2,1,0:T(1,128)} %param.12), calls=%async_computation.1 | async-start | bytes 8192 | tf_op jit(solution)/shard_map/all_to_all | solution.py:87
  38.5 5.3 %copy-start = (bf16[2,64,1024]{2,1,0:T(8,128)(2,1)S(1)}, bf16[2,64,1024]{2,1,0:T(8,128)(2,1)}, u32[]{:S(2)}) copy-start(bf16[2,64,1024]{2,1,0:T(8,128)(2,1)} %param.8) | copy-start | bytes 786436
  40.5 9.7 %all-to-all-start.2 = ((bf16[8,1,16]{2,1,0:T(2,128)(2,1)}), bf16[8,1,16]{2,1,0:T(2,128)(2,1)S(1)}, u32[]{:S(2)}, u32[]{:S(2)}) async-start(bf16[8,1,16]{2,1,0:T(2,128)(2,1)} %copy.47), calls=%async_computation.2 | async-start | bytes 8192 | tf_op jit(solution)/shard_map/all_to_all | solution.py:95
  50.1 11.6 %all-to-all-start.3 = ((bf16[8,16,1024]{2,1,0:T(8,128)(2,1)}), bf16[8,16,1024]{2,1,0:T(8,128)(2,1)S(1)}, u32[]{:S(2)}, u32[]{:S(2)}) async-start(bf16[8,16,1024]{2,1,0:T(8,128)(2,1)} %broadcast_select_fusion), calls=%async_computation.3 | async-start | bytes 524288 | tf_op jit(solution)/shard_map/all_to_all | solution.py:94
  90.5 9.8 %all-to-all-start.4 = ((f32[8,1,1]{2,1,0:T(1,128)}), f32[8,1,1]{2,1,0:T(1,128)S(1)}, u32[]{:S(2)}, u32[]{:S(2)}) async-start(f32[8,1,1]{2,1,0:T(1,128)} %copy.53), calls=%async_computation.4 | async-start | bytes 8192 | tf_op jit(solution)/shard_map/all_to_all | solution.py:104
Sparse Core Ops, SparseCore 0:
  9.5 19.4 all-gather.4
where the time goes:
time: 108 us
  waiting for transfers between devices  24.2 us (22%)
  starting transfers between devices  23.4 us (22%)
  other arithmetic  16.7 us (15%)
  blocking collectives  15.4 us (14%)
  between operations  14.3 us (13%)
  local copies, waits for them, and re-layouts  13.5 us (12%)
    top_k x1, other arithmetic, one_group(): lowest = -lax.top_k(-dist, 2)[0]  10.5 us
    all_gather x2, blocking collectives, joined(): everything = jax.tree.map(lambda part: lax.all_gather(part, axis), shard)  10.4 us
    all_to_all x1, starting transfers between devices, on_device(): lax.all_to_all(second_local, 'img', split_axis=0, concat_axis=0, tiled=True)  7.31 us
    all_to_all x1, waiting for transfers between devices, on_device(): lax.all_to_all(blocks, 'img', split_axis=0, concat_axis=0, tiled=True)  7.07 us
    all_to_all x1, waiting for transfers between devices, on_device(): lax.all_to_all(lists, 'img', split_axis=0, concat_axis=0, tiled=True)  6.02 us
    all_to_all x1, starting transfers between devices, on_device(): lax.all_to_all(lists, 'img', split_axis=0, concat_axis=0, tiled=True)  6.01 us
    all_to_all x1, waiting for transfers between devices, on_device(): lax.all_to_all(score, 'img', split_axis=0, concat_axis=0, tiled=True)  5.81 us
    all_gather x1, blocking collectives, on_device(): lax.all_gather(cell_counts.astype(jnp.bfloat16), 'rep', axis=1, tiled=True)  5.05 us
  transfers between devices with their start and end apart: 6, of which 4 were waited for; matrix products, arithmetic and copies ran while one was open for 9% of the time, Pallas kernels for 0%

commit v1 on v0

--- a/solution.py
+++ b/solution.py
@@ -7,6 +7,28 @@
 KP = 8
 distant = 1000000000.0
 group_size = 8
+
+
+def cut_along(shard, dim, length):
+    before, after = (shard.shape[:dim], shard.shape[dim + 1 :])
+    return jnp.moveaxis(shard.reshape(*before, length, -1, *after), dim, 0)
+
+
+def laid_out(blocks, dim):
+    blocks = jnp.moveaxis(blocks, 0, dim)
+    dims = blocks.shape
+    return blocks.reshape(*dims[:dim], dims[dim] * dims[dim + 1], *dims[dim + 2 :])
+
+
+def rotated_exchange(value, axis, split_dim, concat_dim):
+    peers, index = (lax.axis_size(axis), lax.axis_index(axis))
+    pieces = cut_along(value, split_dim, peers)
+    done = [pieces[index]]
+    for lap in range(1, peers):
+        sent = pieces[(index + lap) % peers]
+        done.append(lax.ppermute(sent, axis, [(i, (i + lap) % peers) for i in range(peers)]))
+    pieces = jnp.stack(done)[(index - jnp.arange(peers)) % peers]
+    return laid_out(pieces, concat_dim)
 
 
 def joined(shard, axis, combine):
@@ -92,7 +114,7 @@
     block_counts = jnp.take(local_counts, rows).reshape(peers, -1).astype(jnp.bfloat16)
     blocks, block_counts = (
         lax.all_to_all(blocks, "img", split_axis=0, concat_axis=0, tiled=True),
-        lax.all_to_all(block_counts, "img", split_axis=0, concat_axis=0, tiled=True),
+        rotated_exchange(block_counts, "img", 0, 0),
     )
     best, runner = nearest(queries, blocks, block_counts, live_cells)
     best, runner = joined((best, runner), "rep", keep_two)

time: 108 us -> 115 us (1.065)
  starting transfers between devices: 23.4 us -> 30 us
    ppermute x0 -> x7, waiting for transfers between devices: none -> 11 us  [rotated_exchange(): lax.ppermute(sent, axis, [(i, (i + lap) % peers) for i in range(peers)])]
    ppermute x0 -> x7, starting transfers between devices: none -> 7.6 us  [rotated_exchange(): lax.ppermute(sent, axis, [(i, (i + lap) % peers) for i in range(peers)])]
    all_to_all x1, waiting for transfers between devices: 7.07 us -> 0.01 us  [on_device(): lax.all_to_all(blocks, 'img', split_axis=0, concat_axis=0, tiled=True)]
    all_to_all x1 -> x0, waiting for transfers between devices: 4.59 us -> none  [on_device(): lax.all_to_all(block_counts, 'img', split_axis=0, concat_axis=0, tiled=True)]
    all_to_all x1 -> x0, starting transfers between devices: 3.31 us -> none  [on_device(): lax.all_to_all(block_counts, 'img', split_axis=0, concat_axis=0, tiled=True)]
    all_to_all x1, starting transfers between devices: 3.41 us -> 5.42 us  [on_device(): lax.all_to_all(blocks, 'img', split_axis=0, concat_axis=0, tiled=True)]
    unnamed x14 -> x22, local copies, waits for them, and re-layouts: 2.81 us -> 2.96 us
  transfers between devices with their start and end apart: 6 -> 12, of which waited for: 4 -> 4; matrix products, arithmetic and copies ran while one was open for 9% -> 9% of each run, Pallas kernels for 0% -> 0%
where the time goes in v1:
time: 115 us; the launch traced here: 114 us
  starting transfers between devices  30 us (26%)
  waiting for transfers between devices  23.6 us (21%)
  other arithmetic  16.7 us (15%)
  blocking collectives  15.4 us (13%)
  between operations  14.4 us (13%)
  local copies, waits for them, and re-layouts  13.6 us (12%)
    ppermute x7, waiting for transfers between devices, rotated_exchange(): lax.ppermute(sent, axis, [(i, (i + lap) % peers) for i in range(peers)])  11 us
    top_k x1, other arithmetic, one_group(): lowest = -lax.top_k(-dist, 2)[0]  10.5 us
    all_gather x2, blocking collectives, joined(): everything = jax.tree.map(lambda part: lax.all_gather(part, axis), shard)  10.4 us
    ppermute x7, starting transfers between devices, rotated_exchange(): lax.ppermute(sent, axis, [(i, (i + lap) % peers) for i in range(peers)])  7.6 us
    all_to_all x1, starting transfers between devices, on_device(): lax.all_to_all(second_local, 'img', split_axis=0, concat_axis=0, tiled=True)  7.31 us
    all_to_all x1, waiting for transfers between devices, on_device(): lax.all_to_all(lists, 'img', split_axis=0, concat_axis=0, tiled=True)  6.02 us
    all_to_all x1, starting transfers between devices, on_device(): lax.all_to_all(lists, 'img', split_axis=0, concat_axis=0, tiled=True)  6.01 us
    all_to_all x1, waiting for transfers between devices, on_device(): lax.all_to_all(score, 'img', split_axis=0, concat_axis=0, tiled=True)  5.88 us
  transfers between devices with their start and end apart: 12, of which 4 were waited for; matrix products, arithmetic and copies ran while one was open for 9% of the time, Pallas kernels for 0%

profile of v1, /device:TPU:0, one launch (start us, length us, event | category | flops | bytes accessed | tf_op | source)
XLA Modules:
  0.0 114.1 jit_solution(15830332560504911571)
XLA Ops:
  7.2 0.7 all-gather.5.cloned.1.call-update
  7.9 0.7 copy.33
  8.6 7.3 %all-to-all-start = ((s32[8,1,1]{2,1,0:T(1,128)}), s32[8,1,1]{2,1,0:T(1,128)S(1)}, u32[]{:S(2)}, u32[]{:S(2)}) async-start(s32[8,1,1]{2,1,0:T(1,128)} %copy.33), calls=%async_computation | async-start | bytes 8192 | tf_op jit(solution)/shard_map/all_to_all | solution.py:110
  15.9 0.7 copy-done.2
  16.7 0.6 copy-done.4
  17.4 5.0 %all-gather.2 = bf16[4,64,2]{1,2,0:T(2,128)(2,1)S(1)} all-gather(bf16[1,64,2]{1,2,0:T(2,128)(2,1)S(1)} %convert_bitcast_fusion), channel_id=1, replica_groups=mesh['img'=8,'rep'=4] {'rep'}, dimensions={0}, use_global_device_ids=true | all-gather | bytes 1280 | tf_op jit(solution)/shard_map/all_gather | solution.py:90
  22.6 0.7 copy-done.1
  23.4 1.3 %gather_fusion = bf16[128]{0:T(256)(128)(2,1)S(1)} fusion(bf16[512]{0:T(512)(128)(2,1)S(1)} %bitcast.73, s32[1024]{0:T(1024)S(1)} %pad_clamp_fusion.2), kind=kCustom, calls=%fused_computation | custom fusion | bytes 1024 | tf_op jit(solution)/shard_map/jit(_take)/gather | solution.py:99
  24.9 0.2 convert_reduce_fusion
  25.8 6.0 %all-to-all-start.1 = ((s32[8,1,16]{2,1,0:T(1,128)}), s32[8,1,16]{2,1,0:T(1,128)S(1)}, u32[]{:S(2)}, u32[]{:S(2)}) async-start(s32[8,1,16]{2,1,0:T(1,128)} %param.12), calls=%async_computation.1 | async-start | bytes 8192 | tf_op jit(solution)/shard_map/all_to_all | solution.py:109
  31.8 0.2 reduce.1
  32.2 6.0 %all-to-all-done.1 = s32[8,1,16]{2,1,0:T(1,128)S(1)} async-done(((s32[8,1,16]{2,1,0:T(1,128)}), s32[8,1,16]{2,1,0:T(1,128)S(1)}, u32[]{:S(2)}, u32[]{:S(2)}) %all-to-all-start.1) | async-done | bytes 544 | tf_op jit(solution)/shard_map/all_to_all | solution.py:109
  38.2 0.5 broadcast.342
  38.7 0.7 reduce.6
  39.5 1.2 %gather_fusion.1 = s32[128]{0:T(128)S(1)} fusion(s32[128]{0:T(128)S(1)} %reshape.372, s32[1024]{0:T(1024)S(1)} %pad_clamp_fusion.1), kind=kCustom, calls=%fused_computation.1 | custom fusion | bytes 1536 | tf_op jit(solution)/shard_map/jit(_take)/gather | solution.py:114
  40.9 0.6 collective-permute-start.6
  41.6 1.4 %collective-permute-start.5 = (bf16[1,16]{1,0:T(2,128)(2,1)S(1)}, bf16[1,16]{1,0:T(2,128)(2,1)S(1)}, u32[]{:S(2)}, u32[]{:S(2)}) collective-permute-start(bf16[1,16]{1,0:T(2,128)(2,1)S(1)} %get-tuple-element.193), channel_id=1, source_target_pairs={{0,24},{4,28},{8,0},{12,4},{16,8},{20,12},{24,16},{28,20},{1,25},{... | collective-permute-start | bytes 104 | tf_op jit(solution)/shard_map/ppermute | solution.py:29
  43.0 1.5 %collective-permute-start.4 = (bf16[1,16]{1,0:T(2,128)(2,1)S(1)}, bf16[1,16]{1,0:T(2,128)(2,1)S(1)}, u32[]{:S(2)}, u32[]{:S(2)}) collective-permute-start(bf16[1,16]{1,0:T(2,128)(2,1)S(1)} %get-tuple-element.194), channel_id=1, source_target_pairs={{0,20},{4,24},{8,28},{12,0},{16,4},{20,8},{24,12},{28,16},{1,21},{... | collective-permute-start | bytes 104 | tf_op jit(solution)/shard_map/ppermute | solution.py:29
  44.5 1.5 %collective-permute-start.3 = (bf16[1,16]{1,0:T(2,128)(2,1)S(1)}, bf16[1,16]{1,0:T(2,128)(2,1)S(1)}, u32[]{:S(2)}, u32[]{:S(2)}) collective-permute-start(bf16[1,16]{1,0:T(2,128)(2,1)S(1)} %get-tuple-element.195), channel_id=1, source_target_pairs={{0,16},{4,20},{8,24},{12,28},{16,0},{20,4},{24,8},{28,12},{1,17},{... | collective-permute-start | bytes 104 | tf_op jit(solution)/shard_map/ppermute | solution.py:29
  46.0 0.6 collective-permute-start
  46.5 0.9 gather_fusion.4
  47.4 0.8 broadcast_select_fusion
  48.2 5.4 %all-to-all-start.2 = ((bf16[8,16,1024]{2,1,0:T(8,128)(2,1)}), bf16[8,16,1024]{2,1,0:T(8,128)(2,1)S(1)}, u32[]{:S(2)}, u32[]{:S(2)}) async-start(bf16[8,16,1024]{2,1,0:T(8,128)(2,1)} %broadcast_select_fusion), calls=%async_computation.2 | async-start | bytes 524288 | tf_op jit(solution)/shard_map/all_to_all | solution.py:116
  53.6 2.0 %collective-permute-start.1 = (bf16[1,16]{1,0:T(2,128)(2,1)S(1)}, bf16[1,16]{1,0:T(2,128)(2,1)S(1)}, u32[]{:S(2)}, u32[]{:S(2)}) collective-permute-start(bf16[1,16]{1,0:T(2,128)(2,1)S(1)} %get-tuple-element.197), channel_id=1, source_target_pairs={{0,8},{4,12},{8,16},{12,20},{16,24},{20,28},{24,0},{28,4},{1,9},{5... | collective-permute-start | bytes 104 | tf_op jit(solution)/shard_map/ppermute | solution.py:29
  55.7 5.6 %collective-permute-done.1 = bf16[1,16]{1,0:T(2,128)(2,1)S(1)} collective-permute-done((bf16[1,16]{1,0:T(2,128)(2,1)S(1)}, bf16[1,16]{1,0:T(2,128)(2,1)S(1)}, u32[]{:S(2)}, u32[]{:S(2)}) %collective-permute-start.1) | collective-permute-done | bytes 64 | tf_op jit(solution)/shard_map/ppermute | solution.py:29
  61.3 5.4 %collective-permute-done.2 = bf16[1,16]{1,0:T(2,128)(2,1)S(1)} collective-permute-done((bf16[1,16]{1,0:T(2,128)(2,1)S(1)}, bf16[1,16]{1,0:T(2,128)(2,1)S(1)}, u32[]{:S(2)}, u32[]{:S(2)}) %collective-permute-start.2) | collective-permute-done | bytes 64 | tf_op jit(solution)/shard_map/ppermute | solution.py:29
  66.8 0.6 gather_fusion.2
  67.7 0.2 multiply_reduce_fusion
  67.9 2.4 %gather_fusion.3 = bf16[128,1024]{1,0:T(8,128)(2,1)S(1)} fusion(bf16[512,1024]{1,0:T(8,128)(2,1)} %bitcast.75, s32[1024]{0:T(1024)S(1)} %pad_clamp_fusion.2), kind=kCustom, calls=%fused_computation.3 | custom fusion | bytes 524800 | tf_op jit(solution)/shard_map/jit(_take)/gather | solution.py:96
  70.4 0.3 convolution_multiply_fusion
  70.8 2.6 %fusion.5 = f32[8,128,128]{2,1,0:T(8,128)S(1)} fusion(f32[8,128,128]{2,1,0:T(8,128)S(1)} %convolution_multiply_fusion, f32[8,128]{1,0:T(8,128)S(1)} %multiply_reduce_fusion, pred[8,128]{1,0:T(8,128)(4,1)S(1)} %compare_and_fusion, bf16[8,128,128]{2,1,0:T(8,128)(2,1)S(1)} %gather.33, pred[8,128]{1,0:T(8,128)(4,1)S(1)} %broadcast_in_dim.112), kind=kOutput, calls=%fused_computation.13 | output fusion | flops 918655 | bytes 1316864 | tf_op jit(solution)/shard_map/while/body/eval_jaxpr/add | solution.py:65
  73.4 0.2 copy.40
  73.6 10.5 %top_k.9 = (f32[8,128,128]{1,2,0:T(8,128)S(1)}, s32[8,128,128]{1,2,0:T(8,128)}) sort(f32[8,128,128]{1,2,0:T(8,128)S(1)} %copy.40, s32[8,128,128]{1,2,0:T(8,128)S(1)} %iota.26.clone), dimensions={2}, to_apply=%region_2.3 | sort | flops 2228224 | bytes 2097152 | tf_op jit(solution)/shard_map/while/body/eval_jaxpr/top_k | solution.py:67
  84.1 0.2 copy.42
  84.3 0.2 fusion.24
  84.5 0.2 copy.36
  84.7 0.2 copy.34
  84.9 5.2 %all-gather = f32[32,128,1]{1,2,0:T(1,128)S(1)} all-gather(f32[8,128,1]{1,2,0:T(1,128)S(1)} %copy.34), channel_id=2, replica_groups=mesh['img'=8,'rep'=4] {'rep'}, dimensions={0}, use_global_device_ids=true | all-gather | bytes 20480 | tf_op jit(solution)/shard_map/all_gather | solution.py:35
  90.1 5.2 %all-gather.1 = f32[32,128,1]{1,2,0:T(1,128)S(1)} all-gather(f32[8,128,1]{1,2,0:T(1,128)S(1)} %copy.36), channel_id=3, replica_groups=mesh['img'=8,'rep'=4] {'rep'}, dimensions={0}, use_global_device_ids=true | all-gather | bytes 20480 | tf_op jit(solution)/shard_map/all_gather | solution.py:35
  95.4 0.1 select_reduce_fusion
  95.5 0.1 fusion.11
  95.6 0.7 copy.38
  96.3 3.6 %all-to-all-start.3 = ((f32[8,1,1]{2,1,0:T(1,128)}), f32[8,1,1]{2,1,0:T(1,128)S(1)}, u32[]{:S(2)}, u32[]{:S(2)}) async-start(f32[8,1,1]{2,1,0:T(1,128)} %copy.38), calls=%async_computation.3 | async-start | bytes 8192 | tf_op jit(solution)/shard_map/all_to_all | solution.py:126
  100.0 0.6 copy.39
  100.6 5.9 %all-to-all-done.3 = f32[8,1,1]{2,1,0:T(1,128)S(1)} async-done(((f32[8,1,1]{2,1,0:T(1,128)}), f32[8,1,1]{2,1,0:T(1,128)S(1)}, u32[]{:S(2)}, u32[]{:S(2)}) %all-to-all-start.3) | async-done | bytes 64 | tf_op jit(solution)/shard_map/all_to_all | solution.py:126
  106.4 0.1 reduce.3
  106.6 0.1 fusion.12
  106.7 0.5 add.328
  (75 shorter events, 2.5 us)
Async XLA Ops:
  7.2 0.7 copy-start.3
  7.2 60.7 %all-gather.5.cloned.1.call-start = ((), (), s32[]{:S(2)}) async-start(), calls=%async_computation.4 | async-start | bytes 1310720 | tf_op jit(solution)/shard_map/all_gather | solution.py:89
  8.6 17.2 %all-to-all-start = ((s32[8,1,1]{2,1,0:T(1,128)}), s32[8,1,1]{2,1,0:T(1,128)S(1)}, u32[]{:S(2)}, u32[]{:S(2)}) async-start(s32[8,1,1]{2,1,0:T(1,128)} %copy.33), calls=%async_computation | async-start | bytes 8192 | tf_op jit(solution)/shard_map/all_to_all | solution.py:110
  15.9 0.7 copy-start.2
  16.7 0.7 copy-start.4
  22.6 0.7 copy-start.1
  25.8 12.4 %all-to-all-start.1 = ((s32[8,1,16]{2,1,0:T(1,128)}), s32[8,1,16]{2,1,0:T(1,128)S(1)}, u32[]{:S(2)}, u32[]{:S(2)}) async-start(s32[8,1,16]{2,1,0:T(1,128)} %param.12), calls=%async_computation.1 | async-start | bytes 8192 | tf_op jit(solution)/shard_map/all_to_all | solution.py:109
  39.5 7.0 %copy-start = (bf16[2,64,1024]{2,1,0:T(8,128)(2,1)S(1)}, bf16[2,64,1024]{2,1,0:T(8,128)(2,1)}, u32[]{:S(2)}) copy-start(bf16[2,64,1024]{2,1,0:T(8,128)(2,1)} %param.8) | copy-start | bytes 786436
  40.9 25.8 %collective-permute-start.6 = (bf16[1,16]{1,0:T(2,128)(2,1)S(1)}, bf16[1,16]{1,0:T(2,128)(2,1)S(1)}, u32[]{:S(2)}, u32[]{:S(2)}) collective-permute-start(bf16[1,16]{1,0:T(2,128)(2,1)S(1)} %get-tuple-element.192), channel_id=1, source_target_pairs={{0,28},{4,0},{8,4},{12,8},{16,12},{20,16},{24,20},{28,24},{1,29},{... | collective-permute-start | bytes 104 | tf_op jit(solution)/shard_map/ppermute | solution.py:29
  41.6 25.1 %collective-permute-start.5 = (bf16[1,16]{1,0:T(2,128)(2,1)S(1)}, bf16[1,16]{1,0:T(2,128)(2,1)S(1)}, u32[]{:S(2)}, u32[]{:S(2)}) collective-permute-start(bf16[1,16]{1,0:T(2,128)(2,1)S(1)} %get-tuple-element.193), channel_id=1, source_target_pairs={{0,24},{4,28},{8,0},{12,4},{16,8},{20,12},{24,16},{28,20},{1,25},{... | collective-permute-start | bytes 104 | tf_op jit(solution)/shard_map/ppermute | solution.py:29
  43.0 23.7 %collective-permute-start.4 = (bf16[1,16]{1,0:T(2,128)(2,1)S(1)}, bf16[1,16]{1,0:T(2,128)(2,1)S(1)}, u32[]{:S(2)}, u32[]{:S(2)}) collective-permute-start(bf16[1,16]{1,0:T(2,128)(2,1)S(1)} %get-tuple-element.194), channel_id=1, source_target_pairs={{0,20},{4,24},{8,28},{12,0},{16,4},{20,8},{24,12},{28,16},{1,21},{... | collective-permute-start | bytes 104 | tf_op jit(solution)/shard_map/ppermute | solution.py:29
  44.5 22.2 %collective-permute-start.3 = (bf16[1,16]{1,0:T(2,128)(2,1)S(1)}, bf16[1,16]{1,0:T(2,128)(2,1)S(1)}, u32[]{:S(2)}, u32[]{:S(2)}) collective-permute-start(bf16[1,16]{1,0:T(2,128)(2,1)S(1)} %get-tuple-element.195), channel_id=1, source_target_pairs={{0,16},{4,20},{8,24},{12,28},{16,0},{20,4},{24,8},{28,12},{1,17},{... | collective-permute-start | bytes 104 | tf_op jit(solution)/shard_map/ppermute | solution.py:29
  46.0 7.7 %collective-permute-start = (bf16[1,16]{1,0:T(2,128)(2,1)S(1)}, bf16[1,16]{1,0:T(2,128)(2,1)S(1)}, u32[]{:S(2)}, u32[]{:S(2)}) collective-permute-start(bf16[1,16]{1,0:T(2,128)(2,1)S(1)} %get-tuple-element.198), channel_id=1, source_target_pairs={{0,4},{4,8},{8,12},{12,16},{16,20},{20,24},{24,28},{28,0},{1,5},{5... | collective-permute-start | bytes 104 | tf_op jit(solution)/shard_map/ppermute | solution.py:29
  48.2 19.3 %all-to-all-start.2 = ((bf16[8,16,1024]{2,1,0:T(8,128)(2,1)}), bf16[8,16,1024]{2,1,0:T(8,128)(2,1)S(1)}, u32[]{:S(2)}, u32[]{:S(2)}) async-start(bf16[8,16,1024]{2,1,0:T(8,128)(2,1)} %broadcast_select_fusion), calls=%async_computation.2 | async-start | bytes 524288 | tf_op jit(solution)/shard_map/all_to_all | solution.py:116
  53.6 7.7 %collective-permute-start.1 = (bf16[1,16]{1,0:T(2,128)(2,1)S(1)}, bf16[1,16]{1,0:T(2,128)(2,1)S(1)}, u32[]{:S(2)}, u32[]{:S(2)}) collective-permute-start(bf16[1,16]{1,0:T(2,128)(2,1)S(1)} %get-tuple-element.197), channel_id=1, source_target_pairs={{0,8},{4,12},{8,16},{12,20},{16,24},{20,28},{24,0},{28,4},{1,9},{5... | collective-permute-start | bytes 104 | tf_op jit(solution)/shard_map/ppermute | solution.py:29
  61.3 5.4 %collective-permute-start.2 = (bf16[1,16]{1,0:T(2,128)(2,1)S(1)}, bf16[1,16]{1,0:T(2,128)(2,1)S(1)}, u32[]{:S(2)}, u32[]{:S(2)}) collective-permute-start(bf16[1,16]{1,0:T(2,128)(2,1)S(1)} %get-tuple-element.196), channel_id=1, source_target_pairs={{0,12},{4,16},{8,20},{12,24},{16,28},{20,0},{24,4},{28,8},{1,13},{... | collective-permute-start | bytes 104 | tf_op jit(solution)/shard_map/ppermute | solution.py:29
  96.3 10.1 %all-to-all-start.3 = ((f32[8,1,1]{2,1,0:T(1,128)}), f32[8,1,1]{2,1,0:T(1,128)S(1)}, u32[]{:S(2)}, u32[]{:S(2)}) async-start(f32[8,1,1]{2,1,0:T(1,128)} %copy.38), calls=%async_computation.3 | async-start | bytes 8192 | tf_op jit(solution)/shard_map/all_to_all | solution.py:126
Sparse Core Ops, SparseCore 0:
  9.5 19.4 all-gather.4
